TPU v7x, 32 devices: a whole 2x2x4 slice. The times are simulated.
32 devices in a mesh: patch: 2 (over y), exp: 4 (over z), tile: 2 (over x), band: 2 (over core).
Axes of the slice: x: 2, y: 2, z: 4, core: 2. Of those that a mesh axis runs over, the one named last changes fastest.
Arguments:
- images: bfloat16 [4, 2, 64, 128, 128], P(('patch', 'band'), 'tile', 'exp'), parts along dimension 0, may hold values from -6 to 6
- mask_bits: int32 [4, 2, 64, 128, 128], P(('patch', 'band'), 'tile', 'exp'), parts along dimension 0, may hold values from 0 to 7
- inv_var: float32 [4, 2, 64], P(('patch', 'band'), 'tile', 'exp'), parts along dimension 0, may hold values from 0.5 to 4
- routes: int32 [4, 2, 64, 1], P(('patch', 'band'), 'tile', 'exp'), parts along dimension 0, may hold values from 0 to 3; in each aligned block of 16 rows (0 to 15, 16 to 31, ..., all dimensions but the last counted through in order) at most 8 rows name the same one
- block_slot: int32 [4, 2, 64], P(('patch', 'band'), 'tile', 'exp'), parts along dimension 0, may hold values from 0 to 7
- kernel_index: int32 [4, 2, 64], P(('patch', 'band'), 'tile', 'exp'), parts along dimension 0, may hold values from 0 to 63
- coefficients: float32 [64, 3], replicated, may hold values from -4 to 4
Outputs:
- coadd: float32 [4, 512, 2048], P(('patch', 'band'), 'tile', 'exp'), parts along dimension 0
- detection: float32 [1024, 2048], P(('patch', 'tile'), 'exp'), parts along dimension 0
There are 2 independent parts, one for each index of `patch`. A program takes and returns all parts, laid end to end along the dimension named above; an argument that names none is the same for every part. Nothing has to cross between parts.
Inputs may be any that keep to these rules, and one draw needn't show every extreme that they name: Among the 16 sub-blocks of one device for one band and strip (an aligned block of routes), no tile column is named more than 8 times, and some tile column is named exactly 8 times.
All inputs are finite; a program needn't handle non-finite values.
Results may differ from a plain program's by a relative error of at most 0.0039.
Values may be sent and summed in bfloat16 or wider, within the bound.
A program may use at most 128 MiB of HBM per device.

v0:
```python
import jax
import jax.numpy as jnp
from jax import lax
from jax.sharding import PartitionSpec as P

BLOCK = 128
TAPS = 41
BLOCK_ROWS = 2
BLOCK_COLS = 4
kernel_sigmas = (1.0, 2.5, 6.0)


def extended(block, sides, width):
    for axis, dim in sides:
        count = lax.axis_size(axis)
        forward = [(i, i + 1) for i in range(count - 1)]
        backward = [(target, source) for source, target in forward]
        low = lax.ppermute(
            lax.slice_in_dim(block, block.shape[dim] - width, None, axis=dim), axis, forward
        )
        high = lax.ppermute(lax.slice_in_dim(block, 0, width, axis=dim), axis, backward)
        block = jnp.concatenate([low, block, high], axis=dim)
    return block


def usable_share(bits):
    flagged = jnp.bitwise_and(bits, 6) == 6
    suspect = jnp.bitwise_and(bits, 1).astype(jnp.float32)
    return jnp.where(flagged, 0.0, 1.0 - 0.5 * suspect)


def band_matrix(length, half_span):
    rows_here = jnp.arange(length + 2 * half_span, dtype=jnp.int32)[:, None]
    cols_here = jnp.arange(length, dtype=jnp.int32)[None, :]
    offset = (rows_here - cols_here - half_span).astype(jnp.float32)
    inside = jnp.abs(offset) <= half_span
    taps_axis = jnp.arange(-half_span, half_span + 1).astype(jnp.float32)
    result = []
    for spread in kernel_sigmas:
        norm_sum = jnp.sum(jnp.exp(-taps_axis * taps_axis / (2.0 * spread * spread)))
        result.append(
            jnp.where(inside, jnp.exp(-offset * offset / (2.0 * spread * spread)), 0.0) / norm_sum
        )
    return jnp.stack(result)


def local(images, mask_bits, inv_var, routes, block_slot, kernel_index, coefficients):
    peer_count = lax.axis_size("exp")
    held_count = images.shape[2]
    capacity = max(2, 2 * held_count // peer_count)
    slot_count = peer_count * capacity
    pixels = BLOCK * BLOCK
    tile_blocks = BLOCK_ROWS * BLOCK_COLS
    coef_count = coefficients.shape[0]
    usable = usable_share(mask_bits[0, 0])
    inverse = inv_var[0, 0][:, None, None]
    weight = (usable * inverse).astype(jnp.bfloat16).reshape(held_count, pixels)
    weighted = (
        (usable * inverse * images[0, 0].astype(jnp.float32))
        .astype(jnp.bfloat16)
        .reshape(held_count, pixels)
    )
    target = routes[0, 0, :, 0]
    ordinal = jnp.arange(held_count, dtype=jnp.int32)
    same_target = target[:, None] == target[None, :]
    earlier = jnp.sum(
        (same_target & (ordinal[None, :] < ordinal[:, None])).astype(jnp.int32), axis=1
    )
    position = target * capacity + earlier
    placed = jnp.arange(slot_count, dtype=jnp.int32)[:, None] == position[None, :]
    placed_int = placed.astype(jnp.int32)
    slot_block = jnp.sum(placed_int * (block_slot[0, 0] + 1)[None, :], axis=1) - 1
    slot_kernel = jnp.sum(placed_int * kernel_index[0, 0][None, :], axis=1)
    labels = jnp.stack([slot_block, slot_kernel], axis=1).reshape(peer_count, capacity, 2)
    placed_half = placed.astype(jnp.bfloat16)
    send_weight = (
        jnp.dot(placed_half, weight, preferred_element_type=jnp.float32)
        .astype(jnp.bfloat16)
        .reshape(peer_count, capacity, pixels)
    )
    block_ids = jnp.arange(tile_blocks, dtype=jnp.int32)[:, None]
    send_weighted = (
        jnp.dot(placed_half, weighted, preferred_element_type=jnp.float32)
        .astype(jnp.bfloat16)
        .reshape(peer_count, capacity, pixels)
    )
    got_weighted, got_weight, got_labels = (
        lax.all_to_all(send_weighted, "exp", split_axis=0, concat_axis=0, tiled=True),
        lax.all_to_all(send_weight, "exp", split_axis=0, concat_axis=0, tiled=True),
        lax.all_to_all(labels, "exp", split_axis=0, concat_axis=0, tiled=True),
    )
    got_labels = got_labels.reshape(slot_count, 2)
    into_block = block_ids == got_labels[:, 0][None, :]
    kernel_pick = (
        got_labels[:, 1][:, None] == jnp.arange(coef_count, dtype=jnp.int32)[None, :]
    ).astype(jnp.float32)
    slot_mix = jnp.dot(kernel_pick, coefficients, precision=lax.Precision.HIGHEST)
    mixing = slot_mix.T[:, None, :] * into_block.astype(jnp.float32)[None, :, :]
    basis_sum = jnp.einsum(
        "kbp,px->kbx",
        mixing,
        got_weighted.reshape(slot_count, pixels).astype(jnp.float32),
        precision=lax.Precision.HIGHEST,
    )
    depth_sum = jnp.dot(
        into_block.astype(jnp.bfloat16),
        got_weight.reshape(slot_count, pixels),
        preferred_element_type=jnp.float32,
    )
    tile_rows = BLOCK_ROWS * BLOCK
    tile_cols = BLOCK_COLS * BLOCK
    basis_tile = (
        basis_sum.reshape(3, BLOCK_ROWS, BLOCK_COLS, BLOCK, BLOCK)
        .transpose(0, 1, 3, 2, 4)
        .reshape(3, tile_rows, tile_cols)
    )
    depth_tile = (
        depth_sum.reshape(BLOCK_ROWS, BLOCK_COLS, BLOCK, BLOCK)
        .transpose(0, 2, 1, 3)
        .reshape(tile_rows, tile_cols)
    )
    half_span = TAPS // 2
    column_mix = band_matrix(tile_cols, half_span)
    row_mix = band_matrix(tile_rows, half_span).transpose(0, 2, 1)
    framed = extended(basis_tile, (("exp", 2), ("tile", 1)), half_span)
    across = jnp.einsum("kyp,kpc->kyc", framed, column_mix, precision=lax.Precision.HIGHEST)
    matched = jnp.einsum("kry,kyc->rc", row_mix, across, precision=lax.Precision.HIGHEST)
    denominator = 1.0 + depth_tile
    coadded = matched / denominator
    detection = lax.psum(coadded * coadded * denominator, "band")
    return (coadded[None], detection)


def solution(mesh):
    return jax.shard_map(
        local,
        mesh=mesh,
        in_specs=(
            P(("patch", "band"), "tile", "exp", None, None),
            P(("patch", "band"), "tile", "exp", None, None),
            P(("patch", "band"), "tile", "exp"),
            P(("patch", "band"), "tile", "exp", None),
            P(("patch", "band"), "tile", "exp"),
            P(("patch", "band"), "tile", "exp"),
            P(),
        ),
        out_specs=(P(("patch", "band"), "tile", "exp"), P(("patch", "tile"), "exp")),
        check_vma=False,
    )
```

profile of v0, /device:TPU:0, one launch (start us, length us, event | category | flops | bytes accessed | tf_op | source)
XLA Modules:
  0.0 137.2 jit_solution(16599511198700164798)
XLA Ops:
  7.2 0.0 copy-start
  7.2 0.0 copy-start.3
  7.2 0.7 add_bitcast_fusion
  7.9 0.9 convert_reduce_fusion
  8.8 0.7 multiply_add_fusion.1
  9.5 0.7 select_reduce_fusion.1
  10.2 0.1 stack.9
  10.3 0.1 sub.118
  10.4 0.6 copy.15
  11.0 6.3 %all-to-all-start = ((s32[4,8,2]{1,2,0:T(2,128)}), s32[4,8,2]{1,2,0:T(2,128)S(1)}, u32[]{:S(2)}, u32[]{:S(2)}) async-start(s32[4,8,2]{1,2,0:T(2,128)} %copy.15), calls=%async_computation | async-start | bytes 8192 | tf_op jit(solution)/shard_map/all_to_all | solution.py:90
  17.4 1.5 %subtract_select_fusion = f32[1,1,16,128,128]{4,3,2,1,0:T(8,128)S(1)} fusion(s32[1,1,16,128,128]{4,3,2,1,0:T(8,128)} %param.8), kind=kLoop, calls=%fused_computation.36 | loop fusion | flops 1835008 | bytes 2097152 | tf_op jit(solution)/shard_map/jit(_where)/select_n | solution.py:29
  18.8 0.0 copy-start.7
  18.8 0.0 copy-done.3
  18.8 0.1 convert.1
  18.9 0.5 copy-done.7
  19.5 2.4 %fusion = bf16[4,8,16384]{2,1,0:T(8,128)(2,1)} fusion(f32[2,8,128,128]{3,2,1,0:T(8,128)S(1)} %convert.1, f32[2,8,128,128]{3,2,1,0:T(8,128)S(1)} %bitcast.88, f32[16]{0:T(128)S(1)} %bitcast.95, s32[16]{0:T(128)S(1)} %multiply_add_fusion.1), kind=kOutput, calls=%fused_computation.2 | convolution fusion | flops 18088448 | bytes 3145856 | tf_op jit(solution)/shard_map/dot_general | solution.py:83
  21.9 1.1 all-to-all-done
  22.9 4.0 %all-to-all-start.1 = ((bf16[4,8,16384]{2,1,0:T(8,128)(2,1)}), bf16[4,8,16384]{2,1,0:T(8,128)(2,1)S(1)}, u32[]{:S(2)}, u32[]{:S(2)}) async-start(bf16[4,8,16384]{2,1,0:T(8,128)(2,1)} %fusion), calls=%async_computation.1 | async-start | bytes 2097152 | tf_op jit(solution)/shard_map/all_to_all | solution.py:88
  27.0 0.6 exponential_reduce_fusion
  27.6 0.6 exponential_reduce_fusion.1
  28.2 0.6 exponential_reduce_fusion.2
  28.8 1.8 %fusion.1 = bf16[4,8,16384]{2,1,0:T(8,128)(2,1)} fusion(f32[2,8,128,128]{3,2,1,0:T(8,128)S(1)} %bitcast.89, f32[16]{0:T(128)S(1)} %bitcast.96, s32[16]{0:T(128)S(1)} %multiply_add_fusion.1), kind=kOutput, calls=%fused_computation.3 | convolution fusion | flops 17826304 | bytes 2097280 | tf_op jit(solution)/shard_map/dot_general | solution.py:77
  30.6 2.0 %select_divide_fusion.2 = f32[1,552,512]{2,1,0:T(8,128)} fusion(f32[]{:T(128)} %exponential_reduce_fusion.2), kind=kLoop, calls=%fused_computation.26 | loop fusion | flops 2826240 | bytes 1130500 | tf_op jit(solution)/shard_map/div | solution.py:42
  32.6 3.3 %select_divide_fusion = (f32[1,552,512]{2,1,0:T(8,128)}, f32[1,552,512]{2,1,0:T(8,128)}) fusion(f32[]{:T(128)} %exponential_reduce_fusion, f32[]{:T(128)} %exponential_reduce_fusion.1), kind=kLoop, calls=%fused_computation.24 | loop fusion | flops 3674112 | bytes 2261000 | tf_op jit(solution)/shard_map/div | solution.py:42
  36.0 16.2 %all-to-all-done.1 = bf16[4,8,16384]{2,1,0:T(8,128)(2,1)S(1)} async-done(((bf16[4,8,16384]{2,1,0:T(8,128)(2,1)}), bf16[4,8,16384]{2,1,0:T(8,128)(2,1)S(1)}, u32[]{:S(2)}, u32[]{:S(2)}) %all-to-all-start.1) | async-done | bytes 1048608 | tf_op jit(solution)/shard_map/all_to_all | solution.py:88
  52.1 4.3 %all-to-all-start.2 = ((bf16[4,8,16384]{2,1,0:T(8,128)(2,1)}), bf16[4,8,16384]{2,1,0:T(8,128)(2,1)}, u32[]{:S(2)}, u32[]{:S(2)}) async-start(bf16[4,8,16384]{2,1,0:T(8,128)(2,1)} %fusion.1), calls=%async_computation.2 | async-start | bytes 2097152 | tf_op jit(solution)/shard_map/all_to_all | solution.py:89
  56.4 0.0 all-reduce.2.cloned.1.call-start
  56.4 2.2 %select_divide_fusion.3 = (f32[1,296,256]{2,1,0:T(8,128)S(1)}, f32[1,296,256]{2,1,0:T(8,128)}) fusion(f32[]{:T(128)} %exponential_reduce_fusion, f32[]{:T(128)} %exponential_reduce_fusion.1), kind=kLoop, calls=%fused_computation.48 | loop fusion | flops 985088 | bytes 606216 | tf_op jit(solution)/shard_map/div | solution.py:42
  58.6 0.1 reshape.298
  58.7 0.0 copy-done
  58.7 0.2 convolution_bitcast_fusion.2
  58.9 0.1 compare_convert_fusion
  59.0 0.3 copy.27
  59.3 1.5 %convolution_bitcast_fusion = f32[3,2,128,4,128]{4,3,2,1,0:T(4,128)S(1)} fusion(bf16[128,128,32,1,1]{1,0,2,4,3:T(8,128)(2,1)S(1)} %bitcast.91, f32[2,4,32]{2,1,0:T(4,128)S(1)} %compare_convert_fusion, f32[3,32]{1,0:T(4,128)S(1)} %convolution_bitcast_fusion.2), kind=kOutput, calls=%fused_computation.20 | convolution fusion | flops 150995712 | bytes 2622848 | tf_op jit(solution)/shard_map/kbp,px->kbx/dot_general | solution.py:99
  60.8 0.6 reshape.301
  61.4 0.2 fusion.42
  61.6 1.3 collective-permute-start.1
  62.9 4.6 %collective-permute-start = (f32[3,256,20]{2,1,0:T(8,128)S(1)}, f32[3,256,20]{2,1,0:T(8,128)S(1)}, u32[]{:S(2)}, u32[]{:S(2)}) collective-permute-start(f32[3,256,20]{2,1,0:T(8,128)S(1)} %get-tuple-element.6), channel_id=1, source_target_pairs={{0,4},{4,8},{8,12},{1,5},{5,9},{9,13},{2,6},{6,10},{10,14},{3,7},{... | collective-permute-start | bytes 184328 | tf_op jit(solution)/shard_map/ppermute | solution.py:18
  67.5 0.7 select_divide_fusion.5
  68.2 15.4 %collective-permute-done.1 = f32[3,256,20]{2,1,0:T(8,128)S(1)} collective-permute-done((f32[3,256,20]{2,1,0:T(8,128)S(1)}, f32[3,256,20]{2,1,0:T(8,128)S(1)}, u32[]{:S(2)}, u32[]{:S(2)}) %collective-permute-start.1) | collective-permute-done | bytes 61472 | tf_op jit(solution)/shard_map/ppermute | solution.py:21
  83.5 0.0 copy-start.4
  83.6 0.0 collective-permute-done
  83.6 0.0 copy-start.6
  83.6 0.9 pad_maximum_fusion.2
  84.5 0.0 copy-done.4
  84.5 0.0 copy-done.6
  84.5 0.0 copy-start.2
  84.5 1.4 %collective-permute-start.3 = (f32[3,20,552]{2,1,0:T(8,128)}, f32[3,20,552]{2,1,0:T(8,128)}, u32[]{:S(2)}, u32[]{:S(2)}) collective-permute-start(f32[3,20,552]{2,1,0:T(8,128)} %get-tuple-element.5), channel_id=1, source_target_pairs={{2,0},{3,1},{6,4},{7,5},{10,8},{11,9},{14,12},{15,13},{18,16},{19,... | collective-permute-start | bytes 397448 | tf_op jit(solution)/shard_map/ppermute | solution.py:21
  85.9 5.9 %collective-permute-start.2 = (f32[3,20,552]{2,1,0:T(8,128)S(1)}, f32[3,20,552]{2,1,0:T(8,128)}, u32[]{:S(2)}, u32[]{:S(2)}) collective-permute-start(f32[3,20,552]{2,1,0:T(8,128)S(1)} %get-tuple-element.4), channel_id=1, source_target_pairs={{0,2},{1,3},{4,6},{5,7},{8,10},{9,11},{12,14},{13,15},{16,18},{17,... | collective-permute-start | bytes 397448 | tf_op jit(solution)/shard_map/ppermute | solution.py:18
  91.8 0.0 all-to-all-done.2
  91.8 0.0 copy-start.5
  91.8 1.6 %convolution_add_fusion = f32[2,4,128,128]{3,1,2,0:T(4,128)S(1)} fusion(s32[32]{0:T(128)S(1)} %get-tuple-element.9, s32[2,4]{1,0:T(2,128)S(1)} %multiply_add_fusion, bf16[4,8,16384]{2,1,0:T(8,128)(2,1)} %all-to-all-done.2), kind=kOutput, calls=%fused_computation.22 | convolution fusion | flops 8519936 | bytes 1573024 | tf_op jit(solution)/shard_map/dot_general | solution.py:105
  93.4 0.0 collective-permute-done.3
  93.4 0.7 collective-permute-done.2
  94.1 0.0 copy-done.2
  94.2 0.0 copy-done.5
  94.2 0.0 copy-start.1
  94.2 6.7 %fusion.2 = f32[3,296,512]{2,1,0:T(8,128)S(1)} fusion(f32[1,552,512]{2,1,0:T(8,128)} %get-tuple-element.12, f32[1,552,512]{2,1,0:T(8,128)} %get-tuple-element.13, f32[1,552,512]{2,1,0:T(8,128)S(1)} %copy-done.2, f32[3,20,552]{2,1,0:T(8,128)} %collective-permute-done.3, f32[3,256,20]{2,1,0:T(8,128)S(1)} %copy-done.5, f32[3,256,512]{2,1,0:T(8,128)S(1)} %reshape.301, ...), kind=kOutput, calls=%fused_computation.4 | convolution fusion | flops 3015297792 | bytes 7170816 | tf_op jit(solution)/shard_map/kyp,kpc->kyc/dot_general | solution.py:126
  100.8 0.0 copy-done.1
  100.8 2.9 %bitcast_multiply_fusion.2 = (f32[256,512]{1,0:T(8,128)}, f32[256,512]{1,0:T(8,128)}) fusion(f32[32,8,4,128]{3,2,1,0:T(4,128)S(1)} %bitcast.92, f32[3,296,512]{2,1,0:T(8,128)S(1)} %fusion.2, f32[1,296,256]{2,1,0:T(8,128)S(1)} %get-tuple-element.14, f32[1,296,256]{2,1,0:T(8,128)S(1)} %copy-done.1, f32[1,296,256]{2,1,0:T(8,128)S(1)} %select_divide_fusion.5), kind=kOutput, calls=%fused_computation.44 | convolution fusion | flops 1397551104 | bytes 4300800 | tf_op jit(solution)/shard_map/kry,kyc->rc/dot_general | solution.py:127
  103.8 0.0 all-reduce.2.cloned.1.call-update
  103.8 24.6 %all-reduce.2.cloned.1.call-done = f32[256,512]{1,0:T(8,128)} async-done(((f32[256,512]{1,0:T(8,128)}), f32[256,512]{1,0:T(8,128)}) %all-reduce.2.cloned.1.call-update) | async-done | bytes 524304 | tf_op jit(solution)/shard_map/psum | solution.py:130
  128.4 1.9 %copy.47 = f32[256,512]{1,0:T(8,128)} copy(f32[256,512]{1,0:T(8,128)} %all-reduce.2.cloned.1.call-done) | data formatting | bytes 1048576
  (5 shorter events, 0.0 us)
Async XLA Ops:
  7.2 51.6 %copy-start = (f32[64,3]{0,1:T(4,128)S(1)}, f32[64,3]{0,1:T(4,128)}, u32[]{:S(2)}) copy-start(f32[64,3]{0,1:T(4,128)} %param.13) | copy-start | bytes 2308
  7.2 11.7 %copy-start.3 = (bf16[1,1,16,128,128]{4,3,2,1,0:T(8,128)(2,1)S(1)}, bf16[1,1,16,128,128]{4,3,2,1,0:T(8,128)(2,1)}, u32[]{:S(2)}) copy-start(bf16[1,1,16,128,128]{4,3,2,1,0:T(8,128)(2,1)} %param.7) | copy-start | bytes 1572868
  11.0 11.9 %all-to-all-start = ((s32[4,8,2]{1,2,0:T(2,128)}), s32[4,8,2]{1,2,0:T(2,128)S(1)}, u32[]{:S(2)}, u32[]{:S(2)}) async-start(s32[4,8,2]{1,2,0:T(2,128)} %copy.15), calls=%async_computation | async-start | bytes 8192 | tf_op jit(solution)/shard_map/all_to_all | solution.py:90
  18.8 0.7 copy-start.7
  22.9 29.2 %all-to-all-start.1 = ((bf16[4,8,16384]{2,1,0:T(8,128)(2,1)}), bf16[4,8,16384]{2,1,0:T(8,128)(2,1)S(1)}, u32[]{:S(2)}, u32[]{:S(2)}) async-start(bf16[4,8,16384]{2,1,0:T(8,128)(2,1)} %fusion), calls=%async_computation.1 | async-start | bytes 2097152 | tf_op jit(solution)/shard_map/all_to_all | solution.py:88
  52.1 39.7 %all-to-all-start.2 = ((bf16[4,8,16384]{2,1,0:T(8,128)(2,1)}), bf16[4,8,16384]{2,1,0:T(8,128)(2,1)}, u32[]{:S(2)}, u32[]{:S(2)}) async-start(bf16[4,8,16384]{2,1,0:T(8,128)(2,1)} %fusion.1), calls=%async_computation.2 | async-start | bytes 2097152 | tf_op jit(solution)/shard_map/all_to_all | solution.py:89
  56.4 72.0 %all-reduce.2.cloned.1.call-start = ((), (), s32[]{:S(2)}) async-start(), calls=%async_computation.3 | async-start | bytes 1048576 | tf_op jit(solution)/shard_map/psum | solution.py:130
  61.6 22.0 %collective-permute-start.1 = (f32[3,256,20]{2,1,0:T(8,128)S(1)}, f32[3,256,20]{2,1,0:T(8,128)S(1)}, u32[]{:S(2)}, u32[]{:S(2)}) collective-permute-start(f32[3,256,20]{2,1,0:T(8,128)S(1)} %get-tuple-element.7), channel_id=1, source_target_pairs={{4,0},{8,4},{12,8},{5,1},{9,5},{13,9},{6,2},{10,6},{14,10},{7,3},{... | collective-permute-start | bytes 184328 | tf_op jit(solution)/shard_map/ppermute | solution.py:21
  62.9 20.7 %collective-permute-start = (f32[3,256,20]{2,1,0:T(8,128)S(1)}, f32[3,256,20]{2,1,0:T(8,128)S(1)}, u32[]{:S(2)}, u32[]{:S(2)}) collective-permute-start(f32[3,256,20]{2,1,0:T(8,128)S(1)} %get-tuple-element.6), channel_id=1, source_target_pairs={{0,4},{4,8},{8,12},{1,5},{5,9},{9,13},{2,6},{6,10},{10,14},{3,7},{... | collective-permute-start | bytes 184328 | tf_op jit(solution)/shard_map/ppermute | solution.py:18
  83.5 0.9 copy-start.4
  83.6 0.9 copy-start.6
  84.5 9.7 %copy-start.2 = (f32[1,552,512]{2,1,0:T(8,128)S(1)}, f32[1,552,512]{2,1,0:T(8,128)}, u32[]{:S(2)}) copy-start(f32[1,552,512]{2,1,0:T(8,128)} %select_divide_fusion.2) | copy-start | bytes 3391492
  84.5 8.9 %collective-permute-start.3 = (f32[3,20,552]{2,1,0:T(8,128)}, f32[3,20,552]{2,1,0:T(8,128)}, u32[]{:S(2)}, u32[]{:S(2)}) collective-permute-start(f32[3,20,552]{2,1,0:T(8,128)} %get-tuple-element.5), channel_id=1, source_target_pairs={{2,0},{3,1},{6,4},{7,5},{10,8},{11,9},{14,12},{15,13},{18,16},{19,... | collective-permute-start | bytes 397448 | tf_op jit(solution)/shard_map/ppermute | solution.py:21
  85.9 8.2 %collective-permute-start.2 = (f32[3,20,552]{2,1,0:T(8,128)S(1)}, f32[3,20,552]{2,1,0:T(8,128)}, u32[]{:S(2)}, u32[]{:S(2)}) collective-permute-start(f32[3,20,552]{2,1,0:T(8,128)S(1)} %get-tuple-element.4), channel_id=1, source_target_pairs={{0,2},{1,3},{4,6},{5,7},{8,10},{9,11},{12,14},{13,15},{16,18},{17,... | collective-permute-start | bytes 397448 | tf_op jit(solution)/shard_map/ppermute | solution.py:18
  91.8 2.4 %copy-start.5 = (f32[3,256,20]{2,1,0:T(8,128)S(1)}, f32[3,256,20]{2,1,0:T(8,128)}, u32[]{:S(2)}) copy-start(f32[3,256,20]{2,1,0:T(8,128)} %copy-done.4) | copy-start | bytes 184324
  94.2 6.7 %copy-start.1 = (f32[1,296,256]{2,1,0:T(8,128)S(1)}, f32[1,296,256]{2,1,0:T(8,128)}, u32[]{:S(2)}) copy-start(f32[1,296,256]{2,1,0:T(8,128)} %get-tuple-element.15) | copy-start | bytes 909316
Sparse Core Ops, SparseCore 0:
  103.9 24.4 all-reduce.1
where the time goes:
time: 138 us; the launch traced here: 137 us
  waiting for transfers between devices  58 us (42%)
  starting transfers between devices  27.8 us (20%)
  matrix products  17 us (12%)
  other arithmetic  15.7 us (11%)
  between operations  14.2 us (10%)
  local copies, waits for them, and re-layouts  4.37 us (3%)
    psum x1, waiting for transfers between devices, local(): detection = lax.psum(coadded * coadded * denominator, 'band')  24.6 us
    all_to_all x1, waiting for transfers between devices, local(): lax.all_to_all(send_weighted, 'exp', split_axis=0, concat_axis=0, tiled=T...  16.2 us
    ppermute x2, waiting for transfers between devices, extended(): lax.ppermute(lax.slice_in_dim(block, 0, width, axis=dim), axis, backward)  15.4 us
    ppermute x2, starting transfers between devices, extended(): lax.ppermute(lax.slice_in_dim(block, block.shape[dim] - width, None, axis...  10.5 us
    div x4, other arithmetic, band_matrix(): jnp.where(inside, jnp.exp(-offset * offset / (2.0 * spread * spread)), 0.0)  8.28 us
    dot_general x1, matrix products, local(): jnp.einsum('kyp,kpc->kyc', framed, column_mix, precision=lax.Precision.HI...  6.67 us
    all_to_all x1, starting transfers between devices, local(): lax.all_to_all(labels, 'exp', split_axis=0, concat_axis=0, tiled=True)  6.35 us
    all_to_all x1, starting transfers between devices, local(): lax.all_to_all(send_weight, 'exp', split_axis=0, concat_axis=0, tiled=True)  4.26 us
  transfers between devices with their start and end apart: 8, of which 5 were waited for; matrix products, arithmetic and copies ran while one was open for 16% of the time, Pallas kernels for 0%

commit v1 on v0

--- a/solution.py
+++ b/solution.py
@@ -127,7 +127,9 @@
     matched = jnp.einsum("kry,kyc->rc", row_mix, across, precision=lax.Precision.HIGHEST)
     denominator = 1.0 + depth_tile
     coadded = matched / denominator
-    detection = lax.psum(coadded * coadded * denominator, "band")
+    incoming_x = coadded * coadded * denominator
+    arr_next = lax.all_gather(incoming_x, axis_name="band")
+    detection = jnp.sum(arr_next, 0)
     return (coadded[None], detection)
 
 

time: 138 us -> 128 us (0.928)
  waiting for transfers between devices: 58 us -> 48.4 us
  other arithmetic: 15.7 us -> 17.9 us
  local copies, waits for them, and re-layouts: 4.37 us -> 2.5 us
    psum x1 -> x0, waiting for transfers between devices: 24.6 us -> none  [local(): detection = lax.psum(coadded * coadded * denominator, 'band')]
    all_gather x0 -> x1, waiting for transfers between devices: none -> 15.1 us  [local(): arr_next = lax.all_gather(incoming_x, axis_name='band')]
    reduce_sum x0 -> x1, other arithmetic: none -> 2.15 us  [local(): detection = jnp.sum(arr_next, 0)]
    unnamed x18 -> x17, local copies, waits for them, and re-layouts: 2.69 us -> 0.82 us
  transfers between devices with their start and end apart: 8 -> 8, of which waited for: 5 -> 5; matrix products, arithmetic and copies ran while one was open for 16% -> 17% of each run, Pallas kernels for 0% -> 0%
where the time goes in v1:
time: 128 us
  waiting for transfers between devices  48.4 us (38%)
  starting transfers between devices  27.8 us (22%)
  other arithmetic  17.9 us (14%)
  matrix products  17 us (13%)
  between operations  14.2 us (11%)
  local copies, waits for them, and re-layouts  2.5 us (2%)
    all_to_all x1, waiting for transfers between devices, local(): lax.all_to_all(send_weighted, 'exp', split_axis=0, concat_axis=0, tiled=T...  16.2 us
    ppermute x2, waiting for transfers between devices, extended(): lax.ppermute(lax.slice_in_dim(block, 0, width, axis=dim), axis, backward)  15.4 us
    all_gather x1, waiting for transfers between devices, local(): arr_next = lax.all_gather(incoming_x, axis_name='band')  15.1 us
    ppermute x2, starting transfers between devices, extended(): lax.ppermute(lax.slice_in_dim(block, block.shape[dim] - width, None, axis...  10.5 us
    div x4, other arithmetic, band_matrix(): jnp.where(inside, jnp.exp(-offset * offset / (2.0 * spread * spread)), 0.0)  8.28 us
    dot_general x1, matrix products, local(): jnp.einsum('kyp,kpc->kyc', framed, column_mix, precision=lax.Precision.HI...  6.67 us
    all_to_all x1, starting transfers between devices, local(): lax.all_to_all(labels, 'exp', split_axis=0, concat_axis=0, tiled=True)  6.35 us
    all_to_all x1, starting transfers between devices, local(): lax.all_to_all(send_weight, 'exp', split_axis=0, concat_axis=0, tiled=True)  4.26 us
  transfers between devices with their start and end apart: 8, of which 5 were waited for; matrix products, arithmetic and copies ran while one was open for 17% of the time, Pallas kernels for 0%

profile of v1, /device:TPU:0, one launch (start us, length us, event | category | flops | bytes accessed | tf_op | source)
XLA Modules:
  0.0 127.9 jit_solution(11652422522278614923)
XLA Ops:
  7.2 0.0 copy-start
  7.2 0.0 copy-start.3
  7.2 0.7 add_bitcast_fusion
  7.9 0.9 convert_reduce_fusion
  8.8 0.7 multiply_add_fusion.1
  9.5 0.7 select_reduce_fusion.1
  10.2 0.1 stack.9
  10.3 0.1 sub.118
  10.4 0.6 copy.15
  11.0 6.3 %all-to-all-start = ((s32[4,8,2]{1,2,0:T(2,128)}), s32[4,8,2]{1,2,0:T(2,128)S(1)}, u32[]{:S(2)}, u32[]{:S(2)}) async-start(s32[4,8,2]{1,2,0:T(2,128)} %copy.15), calls=%async_computation | async-start | bytes 8192 | tf_op jit(solution)/shard_map/all_to_all | solution.py:90
  17.4 1.5 %subtract_select_fusion = f32[1,1,16,128,128]{4,3,2,1,0:T(8,128)S(1)} fusion(s32[1,1,16,128,128]{4,3,2,1,0:T(8,128)} %param.8), kind=kLoop, calls=%fused_computation.36 | loop fusion | flops 1835008 | bytes 2097152 | tf_op jit(solution)/shard_map/jit(_where)/select_n | solution.py:29
  18.8 0.0 copy-start.7
  18.8 0.0 copy-done.3
  18.8 0.1 convert.1
  18.9 0.5 copy-done.7
  19.5 2.4 %fusion = bf16[4,8,16384]{2,1,0:T(8,128)(2,1)} fusion(f32[2,8,128,128]{3,2,1,0:T(8,128)S(1)} %convert.1, f32[2,8,128,128]{3,2,1,0:T(8,128)S(1)} %bitcast.89, f32[16]{0:T(128)S(1)} %bitcast.97, s32[16]{0:T(128)S(1)} %multiply_add_fusion.1), kind=kOutput, calls=%fused_computation.2 | convolution fusion | flops 18088448 | bytes 3145856 | tf_op jit(solution)/shard_map/dot_general | solution.py:83
  21.9 1.1 all-to-all-done
  22.9 4.0 %all-to-all-start.1 = ((bf16[4,8,16384]{2,1,0:T(8,128)(2,1)}), bf16[4,8,16384]{2,1,0:T(8,128)(2,1)S(1)}, u32[]{:S(2)}, u32[]{:S(2)}) async-start(bf16[4,8,16384]{2,1,0:T(8,128)(2,1)} %fusion), calls=%async_computation.1 | async-start | bytes 2097152 | tf_op jit(solution)/shard_map/all_to_all | solution.py:88
  27.0 0.6 exponential_reduce_fusion
  27.6 0.6 exponential_reduce_fusion.1
  28.2 0.6 exponential_reduce_fusion.2
  28.8 1.8 %fusion.1 = bf16[4,8,16384]{2,1,0:T(8,128)(2,1)} fusion(f32[2,8,128,128]{3,2,1,0:T(8,128)S(1)} %bitcast.90, f32[16]{0:T(128)S(1)} %bitcast.98, s32[16]{0:T(128)S(1)} %multiply_add_fusion.1), kind=kOutput, calls=%fused_computation.3 | convolution fusion | flops 17826304 | bytes 2097280 | tf_op jit(solution)/shard_map/dot_general | solution.py:77
  30.6 2.0 %select_divide_fusion.2 = f32[1,552,512]{2,1,0:T(8,128)} fusion(f32[]{:T(128)} %exponential_reduce_fusion.2), kind=kLoop, calls=%fused_computation.26 | loop fusion | flops 2826240 | bytes 1130500 | tf_op jit(solution)/shard_map/div | solution.py:42
  32.6 3.3 %select_divide_fusion = (f32[1,552,512]{2,1,0:T(8,128)}, f32[1,552,512]{2,1,0:T(8,128)}) fusion(f32[]{:T(128)} %exponential_reduce_fusion, f32[]{:T(128)} %exponential_reduce_fusion.1), kind=kLoop, calls=%fused_computation.24 | loop fusion | flops 3674112 | bytes 2261000 | tf_op jit(solution)/shard_map/div | solution.py:42
  36.0 16.2 %all-to-all-done.1 = bf16[4,8,16384]{2,1,0:T(8,128)(2,1)S(1)} async-done(((bf16[4,8,16384]{2,1,0:T(8,128)(2,1)}), bf16[4,8,16384]{2,1,0:T(8,128)(2,1)S(1)}, u32[]{:S(2)}, u32[]{:S(2)}) %all-to-all-start.1) | async-done | bytes 1048608 | tf_op jit(solution)/shard_map/all_to_all | solution.py:88
  52.1 4.3 %all-to-all-start.2 = ((bf16[4,8,16384]{2,1,0:T(8,128)(2,1)}), bf16[4,8,16384]{2,1,0:T(8,128)(2,1)}, u32[]{:S(2)}, u32[]{:S(2)}) async-start(bf16[4,8,16384]{2,1,0:T(8,128)(2,1)} %fusion.1), calls=%async_computation.2 | async-start | bytes 2097152 | tf_op jit(solution)/shard_map/all_to_all | solution.py:89
  56.4 0.0 all-gather.3.cloned.1.call-start
  56.4 2.2 %select_divide_fusion.3 = (f32[1,296,256]{2,1,0:T(8,128)S(1)}, f32[1,296,256]{2,1,0:T(8,128)}) fusion(f32[]{:T(128)} %exponential_reduce_fusion, f32[]{:T(128)} %exponential_reduce_fusion.1), kind=kLoop, calls=%fused_computation.48 | loop fusion | flops 985088 | bytes 606216 | tf_op jit(solution)/shard_map/div | solution.py:42
  58.6 0.1 reshape.298
  58.7 0.0 copy-done
  58.7 0.2 convolution_bitcast_fusion.2
  58.9 0.1 compare_convert_fusion
  59.0 0.3 copy.27
  59.3 1.5 %convolution_bitcast_fusion = f32[3,2,128,4,128]{4,3,2,1,0:T(4,128)S(1)} fusion(bf16[128,128,32,1,1]{1,0,2,4,3:T(8,128)(2,1)S(1)} %bitcast.92, f32[2,4,32]{2,1,0:T(4,128)S(1)} %compare_convert_fusion, f32[3,32]{1,0:T(4,128)S(1)} %convolution_bitcast_fusion.2), kind=kOutput, calls=%fused_computation.20 | convolution fusion | flops 150995712 | bytes 2622848 | tf_op jit(solution)/shard_map/kbp,px->kbx/dot_general | solution.py:99
  60.8 0.6 reshape.301
  61.4 0.2 fusion.42
  61.6 1.3 %collective-permute-start.1 = (f32[3,256,20]{2,1,0:T(8,128)S(1)}, f32[3,256,20]{2,1,0:T(8,128)S(1)}, u32[]{:S(2)}, u32[]{:S(2)}) collective-permute-start(f32[3,256,20]{2,1,0:T(8,128)S(1)} %get-tuple-element.7), channel_id=1, source_target_pairs={{4,0},{8,4},{12,8},{5,1},{9,5},{13,9},{6,2},{10,6},{14,10},{7,3},{... | collective-permute-start | bytes 184328 | tf_op jit(solution)/shard_map/ppermute | solution.py:21
  62.9 4.6 %collective-permute-start = (f32[3,256,20]{2,1,0:T(8,128)S(1)}, f32[3,256,20]{2,1,0:T(8,128)S(1)}, u32[]{:S(2)}, u32[]{:S(2)}) collective-permute-start(f32[3,256,20]{2,1,0:T(8,128)S(1)} %get-tuple-element.6), channel_id=1, source_target_pairs={{0,4},{4,8},{8,12},{1,5},{5,9},{9,13},{2,6},{6,10},{10,14},{3,7},{... | collective-permute-start | bytes 184328 | tf_op jit(solution)/shard_map/ppermute | solution.py:18
  67.5 0.7 select_divide_fusion.5
  68.2 15.4 %collective-permute-done.1 = f32[3,256,20]{2,1,0:T(8,128)S(1)} collective-permute-done((f32[3,256,20]{2,1,0:T(8,128)S(1)}, f32[3,256,20]{2,1,0:T(8,128)S(1)}, u32[]{:S(2)}, u32[]{:S(2)}) %collective-permute-start.1) | collective-permute-done | bytes 61472 | tf_op jit(solution)/shard_map/ppermute | solution.py:21
  83.5 0.0 copy-start.4
  83.6 0.0 collective-permute-done
  83.6 0.0 copy-start.6
  83.6 0.9 pad_maximum_fusion.2
  84.5 0.0 copy-done.4
  84.5 0.0 copy-done.6
  84.5 0.0 copy-start.2
  84.5 1.4 %collective-permute-start.3 = (f32[3,20,552]{2,1,0:T(8,128)}, f32[3,20,552]{2,1,0:T(8,128)}, u32[]{:S(2)}, u32[]{:S(2)}) collective-permute-start(f32[3,20,552]{2,1,0:T(8,128)} %get-tuple-element.5), channel_id=1, source_target_pairs={{2,0},{3,1},{6,4},{7,5},{10,8},{11,9},{14,12},{15,13},{18,16},{19,... | collective-permute-start | bytes 397448 | tf_op jit(solution)/shard_map/ppermute | solution.py:21
  85.9 5.9 %collective-permute-start.2 = (f32[3,20,552]{2,1,0:T(8,128)S(1)}, f32[3,20,552]{2,1,0:T(8,128)}, u32[]{:S(2)}, u32[]{:S(2)}) collective-permute-start(f32[3,20,552]{2,1,0:T(8,128)S(1)} %get-tuple-element.4), channel_id=1, source_target_pairs={{0,2},{1,3},{4,6},{5,7},{8,10},{9,11},{12,14},{13,15},{16,18},{17,... | collective-permute-start | bytes 397448 | tf_op jit(solution)/shard_map/ppermute | solution.py:18
  91.8 0.0 all-to-all-done.2
  91.8 0.0 copy-start.5
  91.8 1.6 %convolution_add_fusion = f32[2,4,128,128]{3,1,2,0:T(4,128)S(1)} fusion(s32[32]{0:T(128)S(1)} %get-tuple-element.9, s32[2,4]{1,0:T(2,128)S(1)} %multiply_add_fusion, bf16[4,8,16384]{2,1,0:T(8,128)(2,1)} %all-to-all-done.2), kind=kOutput, calls=%fused_computation.22 | convolution fusion | flops 8519936 | bytes 1573024 | tf_op jit(solution)/shard_map/dot_general | solution.py:105
  93.4 0.0 collective-permute-done.3
  93.4 0.7 collective-permute-done.2
  94.1 0.0 copy-done.2
  94.2 0.0 copy-done.5
  94.2 0.0 copy-start.1
  94.2 6.7 %fusion.2 = f32[3,296,512]{2,1,0:T(8,128)S(1)} fusion(f32[1,552,512]{2,1,0:T(8,128)} %get-tuple-element.12, f32[1,552,512]{2,1,0:T(8,128)} %get-tuple-element.13, f32[1,552,512]{2,1,0:T(8,128)S(1)} %copy-done.2, f32[3,20,552]{2,1,0:T(8,128)} %collective-permute-done.3, f32[3,256,20]{2,1,0:T(8,128)S(1)} %copy-done.5, f32[3,256,512]{2,1,0:T(8,128)S(1)} %reshape.301, ...), kind=kOutput, calls=%fused_computation.4 | convolution fusion | flops 3015297792 | bytes 7170816 | tf_op jit(solution)/shard_map/kyp,kpc->kyc/dot_general | solution.py:126
  100.8 0.0 copy-done.1
  100.8 2.9 %bitcast_multiply_fusion.2 = (f32[256,512]{1,0:T(8,128)}, f32[256,512]{1,0:T(8,128)}) fusion(f32[32,8,4,128]{3,2,1,0:T(4,128)S(1)} %bitcast.93, f32[3,296,512]{2,1,0:T(8,128)S(1)} %fusion.2, f32[1,296,256]{2,1,0:T(8,128)S(1)} %get-tuple-element.14, f32[1,296,256]{2,1,0:T(8,128)S(1)} %copy-done.1, f32[1,296,256]{2,1,0:T(8,128)S(1)} %select_divide_fusion.5), kind=kOutput, calls=%fused_computation.44 | convolution fusion | flops 1397551104 | bytes 4300800 | tf_op jit(solution)/shard_map/kry,kyc->rc/dot_general | solution.py:127
  103.8 0.0 all-gather.3.cloned.1.call-update
  103.8 15.1 %all-gather.3.cloned.1.call-done = f32[512,512]{1,0:T(8,128)} async-done(((f32[256,512]{1,0:T(8,128)}), f32[512,512]{1,0:T(8,128)}) %all-gather.3.cloned.1.call-update) | async-done | bytes 1048592 | tf_op jit(solution)/shard_map/all_gather | solution.py:131
  118.9 2.1 %reduce_sum.81 = f32[256,512]{1,0:T(8,128)} reduce(f32[2,256,512]{2,1,0:T(8,128)} %bitcast.94, f32[]{:T(128)} %constant.19.clone.1), dimensions={0}, to_apply=%region_6.7 | reduce | flops 131072 | bytes 1572868 | tf_op jit(solution)/shard_map/reduce_sum | solution.py:132
  (5 shorter events, 0.0 us)
Async XLA Ops:
  7.2 51.6 %copy-start = (f32[64,3]{0,1:T(4,128)S(1)}, f32[64,3]{0,1:T(4,128)}, u32[]{:S(2)}) copy-start(f32[64,3]{0,1:T(4,128)} %param.13) | copy-start | bytes 2308
  7.2 11.7 %copy-start.3 = (bf16[1,1,16,128,128]{4,3,2,1,0:T(8,128)(2,1)S(1)}, bf16[1,1,16,128,128]{4,3,2,1,0:T(8,128)(2,1)}, u32[]{:S(2)}) copy-start(bf16[1,1,16,128,128]{4,3,2,1,0:T(8,128)(2,1)} %param.7) | copy-start | bytes 1572868
  11.0 11.9 %all-to-all-start = ((s32[4,8,2]{1,2,0:T(2,128)}), s32[4,8,2]{1,2,0:T(2,128)S(1)}, u32[]{:S(2)}, u32[]{:S(2)}) async-start(s32[4,8,2]{1,2,0:T(2,128)} %copy.15), calls=%async_computation | async-start | bytes 8192 | tf_op jit(solution)/shard_map/all_to_all | solution.py:90
  18.8 0.7 copy-start.7
  22.9 29.2 %all-to-all-start.1 = ((bf16[4,8,16384]{2,1,0:T(8,128)(2,1)}), bf16[4,8,16384]{2,1,0:T(8,128)(2,1)S(1)}, u32[]{:S(2)}, u32[]{:S(2)}) async-start(bf16[4,8,16384]{2,1,0:T(8,128)(2,1)} %fusion), calls=%async_computation.1 | async-start | bytes 2097152 | tf_op jit(solution)/shard_map/all_to_all | solution.py:88
  52.1 39.7 %all-to-all-start.2 = ((bf16[4,8,16384]{2,1,0:T(8,128)(2,1)}), bf16[4,8,16384]{2,1,0:T(8,128)(2,1)}, u32[]{:S(2)}, u32[]{:S(2)}) async-start(bf16[4,8,16384]{2,1,0:T(8,128)(2,1)} %fusion.1), calls=%async_computation.2 | async-start | bytes 2097152 | tf_op jit(solution)/shard_map/all_to_all | solution.py:89
  56.4 62.5 %all-gather.3.cloned.1.call-start = ((), (), s32[]{:S(2)}) async-start(), calls=%async_computation.3 | async-start | bytes 1572864 | tf_op jit(solution)/shard_map/all_gather | solution.py:131
  61.6 22.0 %collective-permute-start.1 = (f32[3,256,20]{2,1,0:T(8,128)S(1)}, f32[3,256,20]{2,1,0:T(8,128)S(1)}, u32[]{:S(2)}, u32[]{:S(2)}) collective-permute-start(f32[3,256,20]{2,1,0:T(8,128)S(1)} %get-tuple-element.7), channel_id=1, source_target_pairs={{4,0},{8,4},{12,8},{5,1},{9,5},{13,9},{6,2},{10,6},{14,10},{7,3},{... | collective-permute-start | bytes 184328 | tf_op jit(solution)/shard_map/ppermute | solution.py:21
  62.9 20.7 %collective-permute-start = (f32[3,256,20]{2,1,0:T(8,128)S(1)}, f32[3,256,20]{2,1,0:T(8,128)S(1)}, u32[]{:S(2)}, u32[]{:S(2)}) collective-permute-start(f32[3,256,20]{2,1,0:T(8,128)S(1)} %get-tuple-element.6), channel_id=1, source_target_pairs={{0,4},{4,8},{8,12},{1,5},{5,9},{9,13},{2,6},{6,10},{10,14},{3,7},{... | collective-permute-start | bytes 184328 | tf_op jit(solution)/shard_map/ppermute | solution.py:18
  83.5 0.9 copy-start.4
  83.6 0.9 copy-start.6
  84.5 9.7 %copy-start.2 = (f32[1,552,512]{2,1,0:T(8,128)S(1)}, f32[1,552,512]{2,1,0:T(8,128)}, u32[]{:S(2)}) copy-start(f32[1,552,512]{2,1,0:T(8,128)} %select_divide_fusion.2) | copy-start | bytes 3391492
  84.5 8.9 %collective-permute-start.3 = (f32[3,20,552]{2,1,0:T(8,128)}, f32[3,20,552]{2,1,0:T(8,128)}, u32[]{:S(2)}, u32[]{:S(2)}) collective-permute-start(f32[3,20,552]{2,1,0:T(8,128)} %get-tuple-element.5), channel_id=1, source_target_pairs={{2,0},{3,1},{6,4},{7,5},{10,8},{11,9},{14,12},{15,13},{18,16},{19,... | collective-permute-start | bytes 397448 | tf_op jit(solution)/shard_map/ppermute | solution.py:21
  85.9 8.2 %collective-permute-start.2 = (f32[3,20,552]{2,1,0:T(8,128)S(1)}, f32[3,20,552]{2,1,0:T(8,128)}, u32[]{:S(2)}, u32[]{:S(2)}) collective-permute-start(f32[3,20,552]{2,1,0:T(8,128)S(1)} %get-tuple-element.4), channel_id=1, source_target_pairs={{0,2},{1,3},{4,6},{5,7},{8,10},{9,11},{12,14},{13,15},{16,18},{17,... | collective-permute-start | bytes 397448 | tf_op jit(solution)/shard_map/ppermute | solution.py:18
  91.8 2.4 %copy-start.5 = (f32[3,256,20]{2,1,0:T(8,128)S(1)}, f32[3,256,20]{2,1,0:T(8,128)}, u32[]{:S(2)}) copy-start(f32[3,256,20]{2,1,0:T(8,128)} %copy-done.4) | copy-start | bytes 184324
  94.2 6.7 %copy-start.1 = (f32[1,296,256]{2,1,0:T(8,128)S(1)}, f32[1,296,256]{2,1,0:T(8,128)}, u32[]{:S(2)}) copy-start(f32[1,296,256]{2,1,0:T(8,128)} %get-tuple-element.15) | copy-start | bytes 909316
Sparse Core Ops, SparseCore 0:
  103.9 14.8 all-gather.2
